TPU v7x, 768 devices: a whole 4x8x12 slice. The times are simulated.
768 devices in a mesh: ctx: 96 (over z, x, core), fsdp: 8 (over y).
Axes of the slice: x: 4, y: 8, z: 12, core: 2. Of those that a mesh axis runs over, the one named last changes fastest.
Arguments:
- projected: bfloat16 [3, 24576, 8192], P(None, 'ctx', 'fsdp'), may hold values from -6 to 6
- short_weight: bfloat16 [3, 3, 8192], P(None, None, 'fsdp'), may hold values from -3 to 3
- rates: float32 [512, 16], P('fsdp'), may hold values from 1.2207031e-05 to 0.03
- residues: float32 [512, 16], P('fsdp'), may hold values from -0.12 to 0.12
- skip: float32 [8192], P('fsdp'), may hold values from -1 to 1
- residual: bfloat16 [24576, 8192], P('ctx', 'fsdp'), may hold values from -40 to 40
- gain: float32 [8192], P('fsdp'), may hold values from 0.5 to 1.5
Outputs:
- new_residual: bfloat16 [24576, 8192], P('ctx', 'fsdp')
- normed: bfloat16 [24576, 8192], P('ctx', 'fsdp')
All inputs are finite; a program needn't handle non-finite values.
Results may differ from a plain program's by a relative error of at most 0.0047.
Values may be sent and summed in bfloat16 or wider, within the bound.
A program may use at most 64 MiB of HBM per device.

v0:
```python
import jax
import jax.numpy as jnp
from jax import lax
from jax.sharding import PartitionSpec as P

CHANNELS_PER_GRP = 16
FILTER_MODES = 16


def passed_along(block, axis, distance):
    devices = range(lax.axis_size(axis))
    route = [(i - distance, i) for i in devices if i - distance in devices]
    return lax.ppermute(block, axis, route)


def per_device(projected, short_weight, rates, residues, skip, residual, gain):
    position = lax.axis_index("ctx")
    block_rows = projected.shape[1]
    width_local = projected.shape[2]
    tap_count = short_weight.shape[0]
    filter_groups = width_local // CHANNELS_PER_GRP
    largest_value = lax.Precision.HIGHEST
    preceding_rows = passed_along(projected[:, block_rows - (tap_count - 1) :, :], "ctx", 1)
    extended = jnp.concatenate([preceding_rows, projected], axis=1).astype(jnp.float32)
    weights = short_weight.astype(jnp.float32)
    filtered = jnp.zeros((3, block_rows, width_local), jnp.float32)
    for shift_amount in range(tap_count):
        lead = tap_count - 1 - shift_amount
        filtered = (
            filtered + weights[shift_amount][:, None, :] * extended[:, lead : lead + block_rows, :]
        )
    query_part = filtered[0]
    product = (filtered[1] * filtered[2]).astype(jnp.bfloat16)
    product_wide = product.astype(jnp.float32)
    sub_rows = min(64, block_rows)
    sub_count = block_rows // sub_rows
    sources = product_wide.reshape(sub_count, sub_rows, filter_groups, CHANNELS_PER_GRP)
    lag_sub = jnp.arange(sub_rows).astype(jnp.float32)
    partial_taps = jnp.sum(
        residues[:, :, None] * jnp.exp(-rates[:, :, None] * lag_sub[None, None, :]), axis=1
    )
    lag_index = jnp.arange(sub_rows)[:, None] - jnp.arange(sub_rows)[None, :]
    causal = lag_index >= 0
    safe_lag = jnp.maximum(lag_index, 0)
    toeplitz = jnp.where(causal[None, :, :], jnp.take(partial_taps, safe_lag, axis=1), 0.0)
    local_conv = jnp.einsum("gts,nsgm->ntgm", toeplitz, sources, precision=largest_value)
    end_sub = jnp.exp(-rates[:, :, None] * (sub_rows - 1 - lag_sub)[None, None, :])
    sub_state = jnp.einsum("grs,nsgm->nrgm", end_sub, sources, precision=largest_value)
    sub_index = jnp.arange(sub_count)
    sub_gap = sub_index[:, None] - 1 - sub_index[None, :]
    sub_valid = sub_gap >= 0
    sub_gap_value = jnp.maximum(sub_gap, 0).astype(jnp.float32)
    mixing = jnp.exp(-rates[:, :, None, None] * (sub_rows * sub_gap_value)[None, None, :, :])
    mixing = jnp.where(sub_valid[None, None, :, :], mixing, 0.0)
    inner_state = jnp.einsum("grji,irgm->jrgm", mixing, sub_state, precision=largest_value)
    tail_decay = jnp.exp(
        -rates[:, :, None]
        * (sub_rows * (sub_count - 1 - sub_index).astype(jnp.float32))[None, None, :]
    )
    state = jnp.einsum("gri,irgm->rgm", tail_decay, sub_state, precision=largest_value).reshape(
        FILTER_MODES, width_local
    )
    rates_modes = rates.T
    piece = lax.all_gather(state[None], "ctx", axis=0, tiled=True)
    count = piece.shape[0]
    lag_blocks = position - 1 - jnp.arange(count)
    valid = lag_blocks >= 0
    lag_value = jnp.maximum(lag_blocks, 0).astype(jnp.float32)
    weight = jnp.exp(-rates_modes[None, :, :] * (block_rows * lag_value)[:, None, None])
    weight = jnp.where(valid[:, None, None], weight, 0.0)
    grouped = piece.reshape(count, FILTER_MODES, filter_groups, CHANNELS_PER_GRP)
    added = jnp.sum(weight[:, :, :, None] * grouped, axis=0)
    carried_state = added.reshape(FILTER_MODES, width_local)
    entry_decay = jnp.exp(
        -rates[:, :, None] * (sub_rows * sub_index.astype(jnp.float32))[None, None, :]
    )
    outer_state = jnp.einsum(
        "grj,rgm->jrgm",
        entry_decay,
        carried_state.reshape(FILTER_MODES, filter_groups, CHANNELS_PER_GRP),
        precision=largest_value,
    )
    incoming_state = inner_state + outer_state
    starting_decay = residues[:, :, None] * jnp.exp(
        -rates[:, :, None] * (lag_sub + 1.0)[None, None, :]
    )
    convolution_carry = jnp.einsum(
        "ixv,qxil->qvil", starting_decay, incoming_state, precision=largest_value
    )
    conv = (local_conv + convolution_carry).reshape(block_rows, width_local)
    summed = residual.astype(jnp.float32) + query_part * (conv + skip[None, :] * product_wide)
    new_residual = summed.astype(jnp.bfloat16)
    squares = lax.psum(jnp.sum(summed * summed, axis=1), "fsdp")
    full_width = width_local * lax.axis_size("fsdp")
    normed = (summed * lax.rsqrt(squares[:, None] / full_width + 1e-05) * gain[None, :]).astype(
        jnp.bfloat16
    )
    return (new_residual, normed)


def solution(mesh):
    return jax.shard_map(
        per_device,
        mesh=mesh,
        in_specs=(
            P(None, "ctx", "fsdp"),
            P(None, None, "fsdp"),
            P("fsdp", None),
            P("fsdp", None),
            P("fsdp"),
            P("ctx", "fsdp"),
            P("fsdp"),
        ),
        out_specs=(P("ctx", "fsdp"), P("ctx", "fsdp")),
        check_vma=False,
    )
```

profile of v0, /device:TPU:6, one launch (start us, length us, event | category | flops | bytes accessed | tf_op | source)
XLA Modules:
  0.0 234.3 jit_solution(8591566055721447228)
XLA Ops:
  7.2 0.0 all-gather.2.cloned.1.call-start
  7.2 0.8 slice.31
  8.0 1.9 collective-permute-start
  10.0 0.7 convert_element_type.75
  10.7 0.7 negate_bitcast_fusion
  11.4 1.2 multiply_exponential_fusion
  12.6 1.7 copy.47
  14.3 0.1 copy.49
  14.4 0.0 collective-permute-done
  14.4 0.4 copy.46
  14.8 1.0 maximum_convert_fusion
  15.8 3.2 %fusion.1 = f32[3,256,1024]{1,2,0:T(8,128)S(1)} fusion(f32[3,258,1024]{1,2,0:T(8,128)S(1)} %maximum_convert_fusion, f32[3,1024]{1,0:T(4,128)S(1)} %get-tuple-element.13, f32[3,1024]{1,0:T(4,128)S(1)} %get-tuple-element.14, f32[3,1024]{1,0:T(4,128)S(1)} %get-tuple-element.12), kind=kLoop, calls=%fused_computation.4 | loop fusion | flops 3932160 | bytes 12619776 | tf_op jit(solution)/shard_map/add | solution.py:30
  19.0 0.9 fusion.17
  19.9 2.8 %convert_element_type.78 = bf16[4,64,64,16]{1,0,3,2:T(4,128)(2,1)} reshape(bf16[1,256,1024]{1,2,0:T(8,128)(2,1)} %fusion.17) | data formatting | bytes 1048576 | tf_op jit(solution)/shard_map/convert_element_type | solution.py:33
  22.6 3.6 %convolution_bitcast_fusion = f32[4,16,64,16]{1,3,0,2:T(8,128)} fusion(bf16[4,64,64,16]{1,0,3,2:T(4,128)(2,1)} %convert_element_type.78, f32[64]{0:T(128)S(1)} %broadcast_subtract_fusion, f32[64,16]{1,0:T(8,128)S(1)} %copy.49), kind=kOutput, calls=%fused_computation.21 | convolution fusion | flops 50397184 | bytes 790784 | tf_op jit(solution)/shard_map/grs,nsgm->nrgm/dot_general | solution.py:48
  26.2 3.7 %copy.54 = f32[4,16,64,16]{3,0,2,1:T(4,128)} copy(f32[4,16,64,16]{1,3,0,2:T(8,128)} %convolution_bitcast_fusion) | data formatting | bytes 524288 | tf_op jit(solution)/shard_map/grs,nsgm->nrgm/transpose | solution.py:48
  30.0 0.0 copy-start.2
  30.0 9.4 %fusion.50 = f32[16,64,1,16]{3,2,1,0:T(1,128)} fusion(f32[64,16,4,1]{2,3,0,1:T(1,128)} %bitcast.66, f32[4,16,64,16]{3,0,2,1:T(4,128)} %copy.54), kind=kOutput, calls=%fused_computation.82 | convolution fusion | flops 786432 | bytes 344064 | tf_op jit(solution)/shard_map/gri,irgm->rgm/dot_general | solution.py:60
  39.4 1.9 broadcast_in_dim_reshape.3
  41.3 0.0 all-gather.2.cloned.1.call-update
  41.3 0.0 copy-done.2
  41.4 0.1 copy.48
  41.4 0.4 multiply_reduce_fusion.1
  41.8 0.1 copy.50
  41.9 0.1 reshape.164
  42.0 14.2 %gather_fusion = f32[4096,64]{1,0:T(8,128)} fusion(f32[64,64]{0,1:T(8,128)S(1)} %copy.50, s32[4096]{0:T(1024)S(1)} %broadcast_clamp_fusion), kind=kCustom, calls=%fused_computation | custom fusion | bytes 2113536 | tf_op jit(solution)/shard_map/jit(_take)/gather | solution.py:45
  56.1 3.8 %copy.51 = f32[64,64,64]{1,0,2:T(8,128)} copy(f32[64,64,64]{2,1,0:T(8,128)} %bitcast.65) | data formatting | bytes 2097152 | tf_op jit(solution)/shard_map/jit(_take)/gather | solution.py:45
  59.9 2.0 copy.45
  62.0 0.1 fusion.44
  62.1 0.1 convert_multiply_fusion.1
  62.2 1.0 exponential_select_fusion
  63.2 104.3 %all-gather.2.cloned.1.call-done = f32[96,16,1024]{2,1,0:T(8,128)} async-done(((f32[1,16,1024]{2,1,0:T(8,128)}), f32[96,16,1024]{2,1,0:T(8,128)}) %all-gather.2.cloned.1.call-update) | async-done | bytes 6291472 | tf_op jit(solution)/shard_map/all_gather | solution.py:64
  167.5 8.2 %copy.55 = f32[96,16,1024]{0,2,1:T(8,128)} copy(f32[96,16,1024]{2,1,0:T(8,128)} %all-gather.2.cloned.1.call-done) | data formatting | bytes 12582912 | tf_op jit(solution)/shard_map/all_gather | solution.py:64
  175.7 5.7 %fusion = f32[16,1024]{1,0:T(8,128)S(1)} fusion(f32[96,16,1024]{0,2,1:T(8,128)} %copy.55, f32[96,16,64]{0,2,1:T(8,128)} %exponential_select_fusion), kind=kLoop, calls=%fused_computation.2 | loop fusion | flops 3129344 | bytes 6750208 | tf_op jit(solution)/shard_map/reduce_sum | solution.py:72
  181.4 1.0 reduce_sum.31
  182.4 9.3 %add_bitcast_fusion.1 = f32[4,16,64,16]{3,0,2,1:T(4,128)S(1)} fusion(f32[4,16,64,16]{3,0,2,1:T(4,128)} %copy.54, f32[16,64,4]{2,1,0:T(8,128)} %get-tuple-element.18, f32[16,64,16]{2,1,0:T(8,128)} %reduce_sum.31, f32[4,4]{1,0:T(4,128)S(1)} %convert_multiply_fusion.1, f32[64,16]{0,1:T(8,128)S(1)} %get-tuple-element.16, pred[4,4]{1,0:T(4,128)(4,1)S(1)} %fusion.44), kind=kOutput, calls=%fused_computation.16 | convolution fusion | flops 3309568 | bytes 610384 | tf_op jit(solution)/shard_map/grji,irgm->jrgm/dot_general | solution.py:55
  191.7 0.0 copy-start
  191.7 0.0 copy-start.1
  191.7 4.7 %fusion.5 = f32[64,4,16,64]{3,2,1,0:T(8,128)S(1)} fusion(f32[4,16,64,16]{3,0,2,1:T(4,128)S(1)} %add_bitcast_fusion.1, f32[64]{0:T(128)S(1)} %broadcast_add_fusion, f32[64,16]{1,0:T(8,128)S(1)} %copy.49, f32[64,16]{1,0:T(8,128)S(1)} %copy.48), kind=kOutput, calls=%fused_computation.11 | convolution fusion | flops 50462720 | bytes 1319168 | tf_op jit(solution)/shard_map/ixv,qxil->qvil/dot_general | solution.py:87
  196.4 0.0 copy-done
  196.4 0.0 copy-done.1
  196.4 2.0 add_bitcast_fusion
  198.5 2.3 copy.57
  200.7 0.0 copy-start.4
  200.7 3.2 %reshape.160 = f32[256,1024]{0,1:T(8,128)} reshape(f32[4,64,64,16]{1,0,3,2:T(4,128)} %copy.57) | data formatting | bytes 2097152 | tf_op jit(solution)/shard_map/reshape | solution.py:90
  204.0 0.0 copy-done.4
  204.0 0.0 copy-start.3
  204.0 2.7 %multiply_reduce_fusion = (f32[256]{0:T(256)S(1)}, f32[256,1024]{0,1:T(8,128)}) fusion(f32[256,1024]{0,1:T(8,128)} %reshape.160, f32[1024]{0:T(1024)S(1)} %copy-done.4, f32[3,256,1024]{1,2,0:T(8,128)S(1)} %fusion.1, bf16[256,1024]{0,1:T(8,128)(2,1)} %copy.45), kind=kLoop, calls=%fused_computation.32 | loop fusion | flops 2621184 | bytes 5772288 | tf_op jit(solution)/shard_map/reduce_sum | solution.py:93
  206.7 17.0 %psum.7 = f32[256]{0:T(256)S(1)} all-reduce(f32[256]{0:T(256)S(1)} %get-tuple-element.8), channel_id=1, replica_groups=mesh['ctx'=96,'fsdp'=8] {'fsdp'}, use_global_device_ids=true, to_apply=%region_3.4 | all-reduce | flops 256 | bytes 2048 | tf_op jit(solution)/shard_map/psum | solution.py:93
  223.7 0.0 copy-done.3
  223.7 1.8 multiply_convert_fusion
  225.5 1.0 copy.58
  226.5 1.0 copy.59
  (12 shorter events, 0.1 us)
Async XLA Ops:
  7.2 160.4 %all-gather.2.cloned.1.call-start = ((), (), s32[]{:S(2)}) async-start(), calls=%async_computation | async-start | bytes 6356992 | tf_op jit(solution)/shard_map/all_gather | solution.py:64
  8.0 6.4 %collective-permute-start = (bf16[3,2,1024]{2,1,0:T(2,128)(2,1)S(1)}, bf16[3,2,1024]{2,1,0:T(2,128)(2,1)S(1)}, u32[]{:S(2)}, u32[]{:S(2)}) collective-permute-start(bf16[3,2,1024]{2,1,0:T(2,128)(2,1)S(1)} %slice.31), channel_id=1, source_target_pairs={{0,8},{8,16},{16,24},{24,32},{32,40},{40,48},{48,56},{56,64},{64,7... | collective-permute-start | bytes 36872 | tf_op jit(solution)/shard_map/ppermute | solution.py:13
  30.0 11.4 %copy-start.2 = (f32[64,16]{0,1:T(8,128)S(1)}, f32[64,16]{0,1:T(8,128)}, u32[]{:S(2)}) copy-start(f32[64,16]{0,1:T(8,128)} %param.10) | copy-start | bytes 12292
  191.7 4.7 %copy-start = (bf16[4,64,64,16]{1,0,3,2:T(4,128)(2,1)S(1)}, bf16[4,64,64,16]{1,0,3,2:T(4,128)(2,1)}, u32[]{:S(2)}) copy-start(bf16[4,64,64,16]{1,0,3,2:T(4,128)(2,1)} %convert_element_type.78) | copy-start | bytes 1572868
  191.7 4.7 %copy-start.1 = (f32[64,64,64]{1,0,2:T(8,128)S(1)}, f32[64,64,64]{1,0,2:T(8,128)}, u32[]{:S(2)}) copy-start(f32[64,64,64]{1,0,2:T(8,128)} %copy.51) | copy-start | bytes 3145732
  200.7 3.2 %copy-start.4 = (f32[1024]{0:T(1024)S(1)}, f32[1024]{0:T(1024)}, u32[]{:S(2)}) copy-start(f32[1024]{0:T(1024)} %param.11) | copy-start | bytes 12292
  204.0 19.7 %copy-start.3 = (f32[1024]{0:T(1024)S(1)}, f32[1024]{0:T(1024)}, u32[]{:S(2)}) copy-start(f32[1024]{0:T(1024)} %param.13) | copy-start | bytes 12292
Sparse Core Ops, SparseCore 0:
  41.5 126.0 all-gather.1
where the time goes:
time: 235 us; the launch traced here: 234 us
  waiting for transfers between devices  104 us (44%)
  local copies, waits for them, and re-layouts  48.4 us (21%)
  matrix products  29 us (12%)
  other arithmetic  19.4 us (8%)
  blocking collectives  17 us (7%)
  between operations  14.2 us (6%)
    all_gather x1, waiting for transfers between devices, per_device(): piece = lax.all_gather(state[None], 'ctx', axis=0, tiled=True)  104 us
    gather x2, local copies, waits for them, and re-layouts, per_device(): jnp.take(partial_taps, safe_lag, axis=1)  18 us
    psum x1, blocking collectives, per_device(): squares = lax.psum(jnp.sum(summed * summed, axis=1), 'fsdp')  17 us
    dot_general x1, matrix products, per_device(): jnp.einsum('gri,irgm->rgm', tail_decay, sub_state, precision=largest_value)  9.38 us
    dot_general x1, matrix products, per_device(): jnp.einsum('grji,irgm->jrgm', mixing, sub_state, precision=largest_value)  9.34 us
    all_gather x1, local copies, waits for them, and re-layouts, per_device(): piece = lax.all_gather(state[None], 'ctx', axis=0, tiled=True)  8.18 us
    unnamed x15, local copies, waits for them, and re-layouts  5.85 us
    reduce_sum x1, other arithmetic, per_device(): added = jnp.sum(weight[:, :, :, None] * grouped, axis=0)  5.66 us
  transfers between devices with their start and end apart: 2, of which 1 were waited for; matrix products, arithmetic and copies ran while one was open for 11% of the time, Pallas kernels for 0%

commit v1 on v0

v1 whole, which is shorter than its diff:
```python
import functools

import jax
import jax.numpy as jnp
from jax import lax
from jax.experimental import pallas as pl
from jax.experimental.pallas import tpu as pltpu
from jax.sharding import PartitionSpec as P

CH = 16
MODES = 16
LANES = 128
GPB = LANES // CH
KB = GPB * MODES
ROW = 8
F32 = jnp.float32
BF16 = jnp.bfloat16
MESH = pl.DeviceIdType.MESH
REACH = 3
LOCAL_A = 4
LOCAL_B = 5


def iota(shape, dim):
    return lax.broadcasted_iota(jnp.int32, shape, dim)


def split(value):
    high = value.astype(BF16)
    return high, (value - high.astype(F32)).astype(BF16)


def mode_column(ref, block):
    groups = ref.shape[1]
    spread = jnp.broadcast_to(ref[...][None], (GPB, MODES, groups)).reshape(KB, groups)
    own = iota((KB, groups), 1) == block * GPB + iota((KB, groups), 0) // MODES
    return jnp.sum(jnp.where(own, spread, 0.0), axis=1, keepdims=True)


def as_row(column):
    same = iota((KB, KB), 0) == iota((KB, KB), 1)
    return jnp.sum(jnp.where(same, jnp.broadcast_to(column, (KB, KB)), 0.0), axis=0, keepdims=True)


def group_mask():
    return iota((KB, LANES), 0) // MODES == iota((KB, LANES), 1) // CH


def by_channel(column):
    spread = jnp.where(group_mask(), jnp.broadcast_to(column, (KB, LANES)), 0.0)
    return jnp.sum(spread.reshape(GPB, MODES, LANES), axis=0)


def short_conv(x, before, taps):
    sub = iota((8, x.shape[1]), 0)
    older, newer = before[0:1, :], before[1:2, :]
    one = pltpu.roll(x, 1, 0)
    two = pltpu.roll(x, 2, 0)
    one_top = jnp.where(sub == 0, newer, one[:8])
    two_top = jnp.where(sub == 0, older, jnp.where(sub == 1, newer, two[:8]))
    one = jnp.concatenate([one_top, one[8:]], axis=0)
    two = jnp.concatenate([two_top, two[8:]], axis=0)
    return taps[0] * x + taps[1] * one + taps[2] * two


def main_kernel(
    nz,
    ny,
    tokens,
    blocks,
    proj_hbm,
    resid_hbm,
    weight_hbm,
    rates_hbm,
    residues_hbm,
    skip_hbm,
    summed_ref,
    inv_ref,
    weight_ref,
    rates_ref,
    residues_ref,
    skip_ref,
    proj,
    resid,
    halo_out,
    halo_in,
    weights,
    p_buf,
    q_buf,
    base_buf,
    e_buf,
    f_buf,
    h_buf,
    edge_buf,
    s_buf,
    rs_buf,
    b_buf,
    c_buf,
    z_buf,
    x_out,
    x_buf,
    sq_acc,
    sq_out,
    sq_buf,
    load_sem,
    halo_sem,
    rs_send,
    rs_recv,
    z_send,
    z_recv,
    x_send,
    x_recv,
    y_send,
    y_recv,
):
    width = blocks * LANES
    ctx = lax.axis_index("ctx")
    y = lax.axis_index("fsdp")
    z = ctx // ROW
    me = ctx % ROW
    last = nz * ROW - 1
    loads = [
        pltpu.make_async_copy(proj_hbm.at[c], proj.at[c], load_sem.at[c]) for c in (1, 2, 0)
    ] + [pltpu.make_async_copy(resid_hbm, resid, load_sem.at[3])]
    small = [
        pltpu.make_async_copy(src, dst, load_sem.at[4 + k])
        for k, (src, dst) in enumerate(
            (
                (rates_hbm, rates_ref),
                (residues_hbm, residues_ref),
                (weight_hbm, weight_ref),
                (skip_hbm, skip_ref),
            )
        )
    ]
    for load in small + loads:
        load.start()
    barrier = pltpu.get_barrier_semaphore()

    def hello(**where):
        pl.semaphore_signal(barrier, inc=1, device_id=where, device_id_type=MESH)

    for k in range(1, REACH + 1):

        @pl.when(z >= k)
        def _():
            hello(ctx=ctx - k * ROW)

    for k in range(1, ROW):
        hello(ctx=z * ROW + (me + k) % ROW)
    for k in range(1, ny):
        hello(fsdp=(y + k) % ny)

    @pl.when(ctx > 0)
    def _():
        hello(ctx=ctx - 1)

    for load in small:
        load.wait()
    weights[...] = weight_ref[...].astype(F32)
    lag = (tokens - 1 - iota((1, tokens), 1)).astype(F32)

    def fill_states(block, carry):
        rate = mode_column(rates_ref, block)
        residue = mode_column(residues_ref, block)
        decay = jnp.exp(-rate * lag)
        high, low = split(decay)
        e_buf[block, pl.ds(0, KB), :] = high
        e_buf[block, pl.ds(KB, KB), :] = low
        edge_buf[block, 0] = by_channel(decay[:, 0:1])
        edge_buf[block, 1] = by_channel(decay[:, 1:2])
        h_buf[block] = jnp.sum((residue * decay).reshape(GPB, MODES, tokens), axis=1)
        return carry

    lax.fori_loop(0, blocks, fill_states, 0)
    for load in loads[:2]:
        load.wait()

    def taps_of(c, cols):
        return [weights[tap, c : c + 1, cols] for tap in range(3)]

    def states(block, carry):
        cols = pl.ds(pl.multiple_of(block * LANES, LANES), LANES)
        none = jnp.zeros((2, LANES), F32)
        key = short_conv(proj[1, :, cols].astype(F32), none, taps_of(1, cols))
        product = key * short_conv(proj[2, :, cols].astype(F32), none, taps_of(2, cols))
        top = jnp.where(iota((8, LANES), 0) < 2, 0.0, product[:8])
        product = jnp.concatenate([top, product[8:]], axis=0).astype(BF16)
        p_buf[block] = product
        both = jnp.dot(e_buf[block], product, preferred_element_type=F32)
        total = jnp.where(group_mask(), both[:KB] + both[KB:], 0.0)
        s_buf[block] = jnp.sum(total.reshape(GPB, MODES, LANES), axis=0)
        return carry

    lax.fori_loop(0, blocks, states, 0)
    loads[2].wait()
    for c in range(3):
        halo_out[c] = proj[c, tokens - 16 :, :].astype(F32)[14:16]

    reach = jnp.minimum(nz - 1 - z, REACH)
    pl.semaphore_wait(barrier, ROW - 1 + ny - 1 + reach + jnp.minimum(last - ctx, 1))

    def halo_copy():
        return pltpu.make_async_remote_copy(
            src_ref=halo_out,
            dst_ref=halo_in,
            send_sem=halo_sem.at[0],
            recv_sem=halo_sem.at[1],
            device_id={"ctx": jnp.minimum(ctx + 1, last)},
            device_id_type=MESH,
        )

    @pl.when(ctx < last)
    def _():
        halo_copy().start()

    @pl.when(ctx == 0)
    def _():
        halo_in[...] = jnp.zeros_like(halo_in)

    @pl.when(ctx > 0)
    def _():
        halo_copy().wait_recv()

    def filtered(c, cols):
        return short_conv(proj[c, :, cols].astype(F32), halo_in[c, :, cols], taps_of(c, cols))

    def first_rows(c):
        every = slice(None)
        return short_conv(proj[c, :16, :].astype(F32), halo_in[c], taps_of(c, every))

    product_top = (first_rows(1) * first_rows(2)).astype(BF16)
    for block in range(blocks):
        top = product_top[:, block * LANES : (block + 1) * LANES]
        p_buf[block, pl.ds(0, 16), :] = top
        wide_top = top.astype(F32)
        s_buf[block] += edge_buf[block, 0] * wide_top[0:1] + edge_buf[block, 1] * wide_top[1:2]

    def rs_copy(k, slot, target):
        return pltpu.make_async_remote_copy(
            src_ref=s_buf.at[target],
            dst_ref=rs_buf.at[slot],
            send_sem=rs_send.at[k],
            recv_sem=rs_recv.at[slot],
            device_id={"ctx": z * ROW + target},
            device_id_type=MESH,
        )

    for k in range(1, ROW):
        rs_copy(k, me, (me + k) % ROW).start()
    rs_buf[me] = s_buf[me]

    loads[3].wait()
    lag_next = (iota((tokens, 1), 0) + 1).astype(F32)

    def local(block, carry):
        cols = pl.ds(pl.multiple_of(block * LANES, LANES), LANES)
        rate = as_row(mode_column(rates_ref, block))
        residue = as_row(mode_column(residues_ref, block))
        high, low = split(residue * jnp.exp(-rate * lag_next))
        f_buf[block, :, pl.ds(0, KB)] = high
        f_buf[block, :, pl.ds(KB, KB)] = low
        product = p_buf[block]
        half = tokens // 2
        lane_group = iota((tokens, LANES), 1) // CH
        causal = iota((half, half), 1) <= iota((half, half), 0)
        taps = h_buf[block]
        total = jnp.zeros((tokens, LANES), F32)
        for g in range(GPB):
            row = jnp.broadcast_to(taps[g : g + 1], (half, tokens))
            rolled = pltpu.roll(row, half + 1, 1, stride=1, stride_axis=0)
            far = rolled[:, :half].astype(BF16)
            near = jnp.where(causal, rolled[:, half:], 0.0).astype(BF16)
            matrix = jnp.concatenate(
                [
                    jnp.concatenate([near, jnp.zeros_like(near)], axis=1),
                    jnp.concatenate([far, near], axis=1),
                ],
                axis=0,
            )
            part = jnp.where(lane_group == g, product, jnp.zeros_like(product))
            total = total + jnp.dot(matrix, part, preferred_element_type=F32)
        query = filtered(0, cols)
        q_buf[block] = query
        wide = product.astype(F32)
        base_buf[block] = resid[:, cols].astype(F32) + query * (total + skip_ref[:, cols] * wide)
        return carry

    lax.fori_loop(0, LOCAL_A, local, 0)

    rate = by_channel(mode_column(rates_ref, me))
    one_block = jnp.exp(-rate * float(tokens))
    one_row = jnp.exp(-rate * float(tokens * ROW))
    for k in range(1, ROW):
        source = (me + ROW - k) % ROW
        rs_copy(k, source, me).wait_recv()
    prefixes = [jnp.zeros((MODES, LANES), F32)]
    for i in range(ROW):
        prefixes.append(one_block * prefixes[-1] + rs_buf[i])
    b_buf[0] = prefixes[ROW]

    def z_copy(k):
        return pltpu.make_async_remote_copy(
            src_ref=b_buf.at[k // REACH],
            dst_ref=z_buf.at[k],
            send_sem=z_send.at[k],
            recv_sem=z_recv.at[k],
            device_id={"ctx": jnp.minimum(ctx + k * ROW, last)},
            device_id_type=MESH,
        )

    for k in range(1, REACH):

        @pl.when(z + k < nz)
        def _():
            z_copy(k).start()

    lax.fori_loop(LOCAL_A, LOCAL_B, local, 0)

    c_buf[...] = jnp.zeros_like(c_buf)
    for k in range(REACH, 0, -1):

        @pl.when(k <= z)
        def _():
            z_copy(k).wait_recv()
            c_buf[...] = one_row * c_buf[...] + z_buf[k]

    entering = c_buf[...]
    b_buf[1] = one_row * entering + prefixes[ROW]

    @pl.when(z + REACH < nz)
    def _():
        z_copy(REACH).start()

    for i in range(ROW):
        value = jnp.exp(-rate * float(tokens * i)) * entering + prefixes[i]
        x_out[i] = value.astype(x_out.dtype)

    def x_copy(k, slot, target):
        return pltpu.make_async_remote_copy(
            src_ref=x_out.at[target],
            dst_ref=x_buf.at[slot],
            send_sem=x_send.at[k],
            recv_sem=x_recv.at[slot],
            device_id={"ctx": z * ROW + target},
            device_id_type=MESH,
        )

    for k in range(1, ROW):
        x_copy(k, me, (me + k) % ROW).start()
    x_buf[me] = x_out[me]
    lax.fori_loop(LOCAL_B, blocks, local, 0)
    sq_acc[...] = jnp.zeros_like(sq_acc)
    for k in range(1, ROW):
        x_copy(k, (me + ROW - k) % ROW, me).wait_recv()

    def finish(block, carry):
        cols = pl.ds(pl.multiple_of(block * LANES, LANES), LANES)
        state = jnp.broadcast_to(x_buf[block].astype(F32)[None], (GPB, MODES, LANES)).reshape(KB, LANES)
        state = jnp.where(group_mask(), state, 0.0).astype(BF16)
        carried = jnp.dot(
            f_buf[block], jnp.concatenate([state, state], axis=0), preferred_element_type=F32
        )
        summed = base_buf[block] + q_buf[block] * carried
        summed_ref[:, cols] = summed
        sq_acc[...] += summed * summed
        return carry

    lax.fori_loop(0, blocks, finish, 0)
    ones = jnp.ones((8, LANES), BF16)
    contract = (((1,), (1,)), ((), ()))
    high, low = split(sq_acc[...])
    squares = lax.dot_general(ones, high, contract, preferred_element_type=F32) + lax.dot_general(
        ones, low, contract, preferred_element_type=F32
    )
    sq_out[...] = squares[:1]

    def y_copy(k, slot, target):
        return pltpu.make_async_remote_copy(
            src_ref=sq_out,
            dst_ref=sq_buf.at[slot],
            send_sem=y_send.at[k],
            recv_sem=y_recv.at[slot],
            device_id={"fsdp": target},
            device_id_type=MESH,
        )

    for k in range(1, ny):
        y_copy(k, y, (y + k) % ny).start()
    sq_buf[y] = sq_out[...]
    for k in range(1, ny):
        y_copy(k, (y + ny - k) % ny, y).wait_recv()
    total = sq_buf[0]
    for k in range(1, ny):
        total = total + sq_buf[k]
    scale = lax.rsqrt(total / float(width * ny) + 1e-05)
    inv_ref[...] = jnp.transpose(jnp.broadcast_to(scale, (LANES, tokens)))

    @pl.when(ctx < last)
    def _():
        halo_copy().wait_send()

    for k in range(1, ROW):
        rs_copy(k, me, (me + k) % ROW).wait_send()
        x_copy(k, me, (me + k) % ROW).wait_send()
    for k in range(1, REACH + 1):

        @pl.when(z + k < nz)
        def _():
            z_copy(k).wait_send()

    for k in range(1, ny):
        y_copy(k, y, (y + k) % ny).wait_send()


def per_device(nz, ny, projected, short_weight, rates, residues, skip, residual, gain):
    tokens, width = residual.shape
    blocks = width // LANES
    vmem = pl.BlockSpec(memory_space=pltpu.VMEM)
    hbm = pl.BlockSpec(memory_space=pltpu.HBM)
    dma = pltpu.SemaphoreType.DMA
    summed, inv = pl.pallas_call(
        functools.partial(main_kernel, nz, ny, tokens, blocks),
        out_shape=(
            jax.ShapeDtypeStruct((tokens, width), F32),
            jax.ShapeDtypeStruct((tokens, LANES), F32),
        ),
        in_specs=[hbm] * 6,
        out_specs=(vmem, vmem),
        scratch_shapes=[
            pltpu.VMEM(short_weight.shape, BF16),
            pltpu.VMEM((MODES, width // CH), F32),
            pltpu.VMEM((MODES, width // CH), F32),
            pltpu.VMEM((1, width), F32),
            pltpu.VMEM((3, tokens, width), BF16),
            pltpu.VMEM((tokens, width), BF16),
            pltpu.VMEM((3, 2, width), F32),
            pltpu.VMEM((3, 2, width), F32),
            pltpu.VMEM((3, 3, width), F32),
            pltpu.VMEM((blocks, tokens, LANES), BF16),
            pltpu.VMEM((blocks, tokens, LANES), F32),
            pltpu.VMEM((blocks, tokens, LANES), F32),
            pltpu.VMEM((blocks, 2 * KB, tokens), BF16),
            pltpu.VMEM((blocks, tokens, 2 * KB), BF16),
            pltpu.VMEM((blocks, GPB, tokens), F32),
            pltpu.VMEM((blocks, 2, MODES, LANES), F32),
            pltpu.VMEM((ROW, MODES, LANES), F32),
            pltpu.VMEM((ROW, MODES, LANES), F32),
            pltpu.VMEM((2, MODES, LANES), F32),
            pltpu.VMEM((MODES, LANES), F32),
            pltpu.VMEM((REACH + 1, MODES, LANES), F32),
            pltpu.VMEM((ROW, MODES, LANES), BF16),
            pltpu.VMEM((ROW, MODES, LANES), BF16),
            pltpu.VMEM((tokens, LANES), F32),
            pltpu.VMEM((1, tokens), F32),
            pltpu.VMEM((ny, 1, tokens), F32),
            dma((8,)),
            dma((2,)),
            dma((ROW,)),
            dma((ROW,)),
            dma((REACH + 1,)),
            dma((REACH + 1,)),
            dma((ROW,)),
            dma((ROW,)),
            dma((ny,)),
            dma((ny,)),
        ],
        compiler_params=pltpu.CompilerParams(
            collective_id=0, has_side_effects=True, vmem_limit_bytes=40 << 20
        ),
        name="scan_conv",
    )(
        *[
            pltpu.with_memory_space_constraint(operand, pltpu.HBM)
            for operand in (
                projected,
                residual,
                short_weight,
                rates.T,
                residues.T,
                skip.reshape(1, width),
            )
        ]
    )
    new_residual = summed.astype(BF16)
    normed = (summed * inv[:, :1] * gain[None, :]).astype(BF16)
    return new_residual, normed


def solution(mesh):
    nz = mesh.shape["ctx"] // ROW
    ny = mesh.shape["fsdp"]
    return jax.shard_map(
        functools.partial(per_device, nz, ny),
        mesh=mesh,
        in_specs=(
            P(None, "ctx", "fsdp"),
            P(None, None, "fsdp"),
            P("fsdp", None),
            P("fsdp", None),
            P("fsdp"),
            P("ctx", "fsdp"),
            P("fsdp"),
        ),
        out_specs=(P("ctx", "fsdp"), P("ctx", "fsdp")),
        check_vma=False,
    )
```

time: 235 us -> 34.9 us (0.15)
  the two profiles are of different devices: /device:TPU:6 before, /device:TPU:704 now
where the time goes in v1:
time: 34.9 us; the launch traced here: 34.7 us
  Pallas kernels  32.8 us (94%)
  other arithmetic  1.14 us (3%)
  between operations  0.66 us (2%)
    pallas_call x1, Pallas kernels, per_device(): pl.pallas_call(functools.partial(main_kernel, nz, ny, tokens, blocks), ou...  32.8 us
    convert_element_type x1, other arithmetic, per_device(): normed = (summed * inv[:, :1] * gain[None, :]).astype(BF16)  1.14 us

profile of v1, /device:TPU:704, one launch (start us, length us, event | category | flops | bytes accessed | tf_op | source)
XLA Modules:
  0.0 34.7 jit_solution(11846940174199199345)
XLA Ops:
  0.6 0.0 copy-start
  0.6 32.8 %scan_conv.1 = (f32[256,1024]{1,0:T(8,128)S(1)}, f32[256,128]{1,0:T(8,128)S(1)}) custom-call(bf16[3,256,1024]{2,1,0:T(8,128)(2,1)} %proj_hbm.1, bf16[256,1024]{1,0:T(8,128)(2,1)} %resid_hbm.1, bf16[3,3,1024]{2,1,0:T(4,128)(2,1)} %weight_hbm.1, f32[16,64]{1,0:T(8,128)} %bitcast.3, f32[16,64]{1,0:T(8,128)} %bitcast.4, f32[1,1024]{1,0:T(1,128)} %bitcast.5), custom_call_target="tpu_custom_call" | custom-call | tf_op jit(solution)/shard_map/scan_conv/pallas_call | solution.py:422
  33.5 0.1 slice_reduce_fusion
  33.6 0.0 copy-done
  33.6 1.1 %multiply_convert_fusion = (bf16[256,1024]{1,0:T(8,128)(2,1)}, bf16[256,1024]{1,0:T(8,128)(2,1)}) fusion(f32[256,1024]{1,0:T(8,128)S(1)} %get-tuple-element.4, f32[1024]{0:T(1024)S(1)} %copy-done, f32[256]{0:T(256)S(1)} %slice_reduce_fusion), kind=kLoop, calls=%fused_computation | loop fusion | flops 1048576 | bytes 2102272 | tf_op jit(solution)/shard_map/convert_element_type | solution.py:486
Async XLA Ops:
  0.6 33.0 %copy-start = (f32[1024]{0:T(1024)S(1)}, f32[1024]{0:T(1024)}, u32[]{:S(2)}) copy-start(f32[1024]{0:T(1024)} %param.13) | copy-start | bytes 12292

commit v2 on v1

--- a/solution.py
+++ b/solution.py
@@ -17,8 +17,9 @@
 BF16 = jnp.bfloat16
 MESH = pl.DeviceIdType.MESH
 REACH = 3
-LOCAL_A = 4
-LOCAL_B = 5
+LOCAL_A = 1
+LOCAL_B = 4
+SENT = MODES + 8
 
 
 def iota(shape, dim):
@@ -92,6 +93,7 @@
     f_buf,
     h_buf,
     edge_buf,
+    edge_in,
     s_buf,
     rs_buf,
     b_buf,
@@ -104,6 +106,8 @@
     sq_buf,
     load_sem,
     halo_sem,
+    edge_send,
+    edge_recv,
     rs_send,
     rs_recv,
     z_send,
@@ -151,9 +155,9 @@
     for k in range(1, ny):
         hello(fsdp=(y + k) % ny)
 
-    @pl.when(ctx > 0)
-    def _():
-        hello(ctx=ctx - 1)
+    @pl.when((z > 0) & (me < ROW - 1))
+    def _():
+        hello(ctx=z * ROW - 1)
 
     for load in small:
         load.wait()
@@ -189,16 +193,55 @@
         p_buf[block] = product
         both = jnp.dot(e_buf[block], product, preferred_element_type=F32)
         total = jnp.where(group_mask(), both[:KB] + both[KB:], 0.0)
-        s_buf[block] = jnp.sum(total.reshape(GPB, MODES, LANES), axis=0)
+        s_buf[block, pl.ds(0, MODES), :] = jnp.sum(total.reshape(GPB, MODES, LANES), axis=0)
         return carry
 
+    for c in (1, 2):
+        tail = proj[c, tokens - 16 :, :].astype(F32)[14:16]
+        head = proj[c, :16, :].astype(F32)[:2]
+        halo_out[c] = tail
+        for block in range(blocks):
+            mine = slice(block * LANES, (block + 1) * LANES)
+            s_buf[block, pl.ds(MODES + 2 * c - 2, 2), :] = tail[:, mine]
+            s_buf[block, pl.ds(MODES + 2 * c + 2, 2), :] = head[:, mine]
     lax.fori_loop(0, blocks, states, 0)
     loads[2].wait()
-    for c in range(3):
-        halo_out[c] = proj[c, tokens - 16 :, :].astype(F32)[14:16]
+    halo_out[0] = proj[0, tokens - 16 :, :].astype(F32)[14:16]
 
     reach = jnp.minimum(nz - 1 - z, REACH)
-    pl.semaphore_wait(barrier, ROW - 1 + ny - 1 + reach + jnp.minimum(last - ctx, 1))
+    fan = jnp.minimum(reach, 1) * (me // (ROW - 1)) * (ROW - 1)
+    pl.semaphore_wait(barrier, ROW - 1 + ny - 1 + reach + fan)
+
+    def rs_copy(k, slot, target):
+        return pltpu.make_async_remote_copy(
+            src_ref=s_buf.at[target],
+            dst_ref=rs_buf.at[slot],
+            send_sem=rs_send.at[k],
+            recv_sem=rs_recv.at[slot],
+            device_id={"ctx": z * ROW + target},
+            device_id_type=MESH,
+        )
+
+    def edge_copy(k):
+        return pltpu.make_async_remote_copy(
+            src_ref=s_buf.at[k, pl.ds(MODES, 8)],
+            dst_ref=edge_in,
+            send_sem=edge_send.at[k],
+            recv_sem=edge_recv,
+            device_id={"ctx": jnp.minimum(z * ROW + ROW + k, last)},
+            device_id_type=MESH,
+        )
+
+    feeds = (me == ROW - 1) & (z < nz - 1)
+
+    @pl.when(feeds)
+    def _():
+        for k in range(ROW):
+            edge_copy(k).start()
+
+    for k in range(1, ROW):
+        rs_copy(k, me, (me + k) % ROW).start()
+    rs_buf[me] = s_buf[me]
 
     def halo_copy():
         return pltpu.make_async_remote_copy(
@@ -231,24 +274,7 @@
 
     product_top = (first_rows(1) * first_rows(2)).astype(BF16)
     for block in range(blocks):
-        top = product_top[:, block * LANES : (block + 1) * LANES]
-        p_buf[block, pl.ds(0, 16), :] = top
-        wide_top = top.astype(F32)
-        s_buf[block] += edge_buf[block, 0] * wide_top[0:1] + edge_buf[block, 1] * wide_top[1:2]
-
-    def rs_copy(k, slot, target):
-        return pltpu.make_async_remote_copy(
-            src_ref=s_buf.at[target],
-            dst_ref=rs_buf.at[slot],
-            send_sem=rs_send.at[k],
-            recv_sem=rs_recv.at[slot],
-            device_id={"ctx": z * ROW + target},
-            device_id_type=MESH,
-        )
-
-    for k in range(1, ROW):
-        rs_copy(k, me, (me + k) % ROW).start()
-    rs_buf[me] = s_buf[me]
+        p_buf[block, pl.ds(0, 16), :] = product_top[:, block * LANES : (block + 1) * LANES]
 
     loads[3].wait()
     lag_next = (iota((tokens, 1), 0) + 1).astype(F32)
@@ -294,9 +320,40 @@
     for k in range(1, ROW):
         source = (me + ROW - k) % ROW
         rs_copy(k, source, me).wait_recv()
+
+    @pl.when(z == 0)
+    def _():
+        edge_in[...] = jnp.zeros_like(edge_in)
+
+    @pl.when(z > 0)
+    def _():
+        edge_copy(0).wait_recv()
+
+    mine = pl.ds(pl.multiple_of(me * LANES, LANES), LANES)
+    key_taps, value_taps = taps_of(1, mine), taps_of(2, mine)
+
+    def first_two(before, at, taps):
+        now = rs_buf[at, pl.ds(MODES + 4, 4), :]
+        out = []
+        for c, w in enumerate(taps):
+            older = before[2 * c : 2 * c + 1]
+            newer = before[2 * c + 1 : 2 * c + 2]
+            first = now[2 * c : 2 * c + 1]
+            second = now[2 * c + 1 : 2 * c + 2]
+            out.append(
+                (
+                    w[0] * first + w[1] * newer + w[2] * older,
+                    w[0] * second + w[1] * first + w[2] * newer,
+                )
+            )
+        return [(out[0][i] * out[1][i]).astype(BF16).astype(F32) for i in range(2)]
+
     prefixes = [jnp.zeros((MODES, LANES), F32)]
     for i in range(ROW):
-        prefixes.append(one_block * prefixes[-1] + rs_buf[i])
+        before = edge_in[:4, :] if i == 0 else rs_buf[i - 1, pl.ds(MODES, 4), :]
+        one, two = first_two(before, i, (key_taps, value_taps))
+        state = rs_buf[i, pl.ds(0, MODES), :] + edge_buf[me, 0] * one + edge_buf[me, 1] * two
+        prefixes.append(one_block * prefixes[-1] + state)
     b_buf[0] = prefixes[ROW]
 
     def z_copy(k):
@@ -399,6 +456,11 @@
     @pl.when(ctx < last)
     def _():
         halo_copy().wait_send()
+
+    @pl.when(feeds)
+    def _():
+        for k in range(ROW):
+            edge_copy(k).wait_send()
 
     for k in range(1, ROW):
         rs_copy(k, me, (me + k) % ROW).wait_send()
@@ -444,8 +506,9 @@
             pltpu.VMEM((blocks, tokens, 2 * KB), BF16),
             pltpu.VMEM((blocks, GPB, tokens), F32),
             pltpu.VMEM((blocks, 2, MODES, LANES), F32),
-            pltpu.VMEM((ROW, MODES, LANES), F32),
-            pltpu.VMEM((ROW, MODES, LANES), F32),
+            pltpu.VMEM((8, LANES), F32),
+            pltpu.VMEM((ROW, SENT, LANES), F32),
+            pltpu.VMEM((ROW, SENT, LANES), F32),
             pltpu.VMEM((2, MODES, LANES), F32),
             pltpu.VMEM((MODES, LANES), F32),
             pltpu.VMEM((REACH + 1, MODES, LANES), F32),
@@ -456,6 +519,8 @@
             pltpu.VMEM((ny, 1, tokens), F32),
             dma((8,)),
             dma((2,)),
+            dma((ROW,)),
+            dma,
             dma((ROW,)),
             dma((ROW,)),
             dma((REACH + 1,)),

time: 34.9 us -> 33.3 us (0.954)
  Pallas kernels: 32.8 us -> 31.3 us
    pallas_call x1, Pallas kernels: 32.8 us -> 31.3 us  [per_device(): pl.pallas_call(functools.partial(main_kernel, nz, ny, tokens, blocks), ou...]
where the time goes in v2:
time: 33.3 us; the launch traced here: 33.2 us
  Pallas kernels  31.3 us (94%)
  other arithmetic  1.14 us (3%)
  between operations  0.66 us (2%)
    pallas_call x1, Pallas kernels, per_device(): pl.pallas_call(functools.partial(main_kernel, nz, ny, tokens, blocks), ou...  31.3 us
    convert_element_type x1, other arithmetic, per_device(): normed = (summed * inv[:, :1] * gain[None, :]).astype(BF16)  1.14 us

profile of v2, /device:TPU:704, one launch (start us, length us, event | category | flops | bytes accessed | tf_op | source)
XLA Modules:
  0.0 33.2 jit_solution(6183296802467351370)
XLA Ops:
  0.6 0.0 copy-start
  0.6 31.3 %scan_conv.1 = (f32[256,1024]{1,0:T(8,128)S(1)}, f32[256,128]{1,0:T(8,128)S(1)}) custom-call(bf16[3,256,1024]{2,1,0:T(8,128)(2,1)} %proj_hbm.1, bf16[256,1024]{1,0:T(8,128)(2,1)} %resid_hbm.1, bf16[3,3,1024]{2,1,0:T(4,128)(2,1)} %weight_hbm.1, f32[16,64]{1,0:T(8,128)} %bitcast.3, f32[16,64]{1,0:T(8,128)} %bitcast.4, f32[1,1024]{1,0:T(1,128)} %bitcast.5), custom_call_target="tpu_custom_call" | custom-call | tf_op jit(solution)/shard_map/scan_conv/pallas_call | solution.py:484
  31.9 0.1 slice_reduce_fusion
  32.0 0.0 copy-done
  32.0 1.1 %multiply_convert_fusion = (bf16[256,1024]{1,0:T(8,128)(2,1)}, bf16[256,1024]{1,0:T(8,128)(2,1)}) fusion(f32[256,1024]{1,0:T(8,128)S(1)} %get-tuple-element.4, f32[1024]{0:T(1024)S(1)} %copy-done, f32[256]{0:T(256)S(1)} %slice_reduce_fusion), kind=kLoop, calls=%fused_computation | loop fusion | flops 1048576 | bytes 2102272 | tf_op jit(solution)/shard_map/convert_element_type | solution.py:551
Async XLA Ops:
  0.6 31.4 %copy-start = (f32[1024]{0:T(1024)S(1)}, f32[1024]{0:T(1024)}, u32[]{:S(2)}) copy-start(f32[1024]{0:T(1024)} %param.13) | copy-start | bytes 12292

commit v3 on v2

--- a/solution.py
+++ b/solution.py
@@ -17,6 +17,7 @@
 BF16 = jnp.bfloat16
 MESH = pl.DeviceIdType.MESH
 REACH = 3
+NEAR = 7
 LOCAL_A = 1
 LOCAL_B = 4
 SENT = MODES + 8
@@ -110,6 +111,8 @@
     edge_recv,
     rs_send,
     rs_recv,
+    ready,
+    f_send,
     z_send,
     z_recv,
     x_send,
@@ -137,7 +140,7 @@
             )
         )
     ]
-    for load in small + loads:
+    for load in small + loads[:2]:
         load.start()
     barrier = pltpu.get_barrier_semaphore()
 
@@ -158,6 +161,13 @@
     @pl.when((z > 0) & (me < ROW - 1))
     def _():
         hello(ctx=z * ROW - 1)
+
+    far = [k for k in range(nz - 1, NEAR, -1)]
+
+    @pl.when(z == 0)
+    def _():
+        for k in far:
+            hello(ctx=me + k * ROW)
 
     for load in small:
         load.wait()
@@ -176,9 +186,11 @@
         h_buf[block] = jnp.sum((residue * decay).reshape(GPB, MODES, tokens), axis=1)
         return carry
 
-    lax.fori_loop(0, blocks, fill_states, 0)
+    lax.fori_loop(0, blocks, fill_states, 0, unroll=True)
     for load in loads[:2]:
         load.wait()
+    for load in loads[2:]:
+        load.start()
 
     def taps_of(c, cols):
         return [weights[tap, c : c + 1, cols] for tap in range(3)]
@@ -204,13 +216,18 @@
             mine = slice(block * LANES, (block + 1) * LANES)
             s_buf[block, pl.ds(MODES + 2 * c - 2, 2), :] = tail[:, mine]
             s_buf[block, pl.ds(MODES + 2 * c + 2, 2), :] = head[:, mine]
-    lax.fori_loop(0, blocks, states, 0)
+    lax.fori_loop(0, blocks, states, 0, unroll=True)
     loads[2].wait()
     halo_out[0] = proj[0, tokens - 16 :, :].astype(F32)[14:16]
 
     reach = jnp.minimum(nz - 1 - z, REACH)
     fan = jnp.minimum(reach, 1) * (me // (ROW - 1)) * (ROW - 1)
-    pl.semaphore_wait(barrier, ROW - 1 + ny - 1 + reach + fan)
+    distant = jnp.minimum(z // (NEAR + 1), 1)
+    pl.semaphore_wait(barrier, ROW - 1 + ny - 1 + reach + fan + distant)
+
+    @pl.when(distant == 1)
+    def _():
+        pl.semaphore_signal(ready.at[z], inc=1, device_id={"ctx": me}, device_id_type=MESH)
 
     def rs_copy(k, slot, target):
         return pltpu.make_async_remote_copy(
@@ -312,7 +329,7 @@
         base_buf[block] = resid[:, cols].astype(F32) + query * (total + skip_ref[:, cols] * wide)
         return carry
 
-    lax.fori_loop(0, LOCAL_A, local, 0)
+    lax.fori_loop(0, LOCAL_A, local, 0, unroll=True)
 
     rate = by_channel(mode_column(rates_ref, me))
     one_block = jnp.exp(-rate * float(tokens))
@@ -366,28 +383,68 @@
             device_id_type=MESH,
         )
 
+    def first_copy(k):
+        return pltpu.make_async_remote_copy(
+            src_ref=b_buf.at[0],
+            dst_ref=z_buf.at[0],
+            send_sem=f_send.at[k],
+            recv_sem=z_recv.at[0],
+            device_id={"ctx": jnp.minimum(me + k * ROW, last)},
+            device_id_type=MESH,
+        )
+
+    def relay_copy():
+        return pltpu.make_async_remote_copy(
+            src_ref=z_buf.at[0],
+            dst_ref=z_buf.at[0],
+            send_sem=z_send.at[0],
+            recv_sem=z_recv.at[0],
+            device_id={"ctx": jnp.minimum(ctx + REACH * ROW, last)},
+            device_id_type=MESH,
+        )
+
+    @pl.when(z == 0)
+    def _():
+        for k in range(1, min(REACH, nz - 1) + 1):
+            first_copy(k).start()
+
     for k in range(1, REACH):
 
-        @pl.when(z + k < nz)
+        @pl.when((z > 0) & (z + k < nz))
         def _():
             z_copy(k).start()
 
-    lax.fori_loop(LOCAL_A, LOCAL_B, local, 0)
+    lax.fori_loop(LOCAL_A, LOCAL_B, local, 0, unroll=True)
 
     c_buf[...] = jnp.zeros_like(c_buf)
     for k in range(REACH, 0, -1):
 
-        @pl.when(k <= z)
+        @pl.when(k < z)
         def _():
             z_copy(k).wait_recv()
             c_buf[...] = one_row * c_buf[...] + z_buf[k]
 
+    chain = c_buf[...]
+    b_buf[1] = one_row * chain + prefixes[ROW]
+
+    @pl.when((z > 0) & (z + REACH < nz))
+    def _():
+        z_copy(REACH).start()
+
+    @pl.when(z > 0)
+    def _():
+        first_copy(1).wait_recv()
+
+    @pl.when((z > 0) & (z + REACH <= min(NEAR, nz - 1)))
+    def _():
+        relay_copy().start()
+
+    @pl.when(z > 0)
+    def _():
+        weight = jnp.exp(-rate * ((z - 1) * (tokens * ROW)).astype(F32))
+        c_buf[...] = chain + weight * z_buf[0]
+
     entering = c_buf[...]
-    b_buf[1] = one_row * entering + prefixes[ROW]
-
-    @pl.when(z + REACH < nz)
-    def _():
-        z_copy(REACH).start()
 
     for i in range(ROW):
         value = jnp.exp(-rate * float(tokens * i)) * entering + prefixes[i]
@@ -406,7 +463,13 @@
     for k in range(1, ROW):
         x_copy(k, me, (me + k) % ROW).start()
     x_buf[me] = x_out[me]
-    lax.fori_loop(LOCAL_B, blocks, local, 0)
+    lax.fori_loop(LOCAL_B, blocks, local, 0, unroll=True)
+    @pl.when(z == 0)
+    def _():
+        for k in far:
+            pl.semaphore_wait(ready.at[k], 1)
+            first_copy(k).start()
+
     sq_acc[...] = jnp.zeros_like(sq_acc)
     for k in range(1, ROW):
         x_copy(k, (me + ROW - k) % ROW, me).wait_recv()
@@ -423,7 +486,7 @@
         sq_acc[...] += summed * summed
         return carry
 
-    lax.fori_loop(0, blocks, finish, 0)
+    lax.fori_loop(0, blocks, finish, 0, unroll=True)
     ones = jnp.ones((8, LANES), BF16)
     contract = (((1,), (1,)), ((), ()))
     high, low = split(sq_acc[...])
@@ -445,6 +508,7 @@
     for k in range(1, ny):
         y_copy(k, y, (y + k) % ny).start()
     sq_buf[y] = sq_out[...]
+
     for k in range(1, ny):
         y_copy(k, (y + ny - k) % ny, y).wait_recv()
     total = sq_buf[0]
@@ -467,9 +531,18 @@
         x_copy(k, me, (me + k) % ROW).wait_send()
     for k in range(1, REACH + 1):
 
-        @pl.when(z + k < nz)
+        @pl.when((z > 0) & (z + k < nz))
         def _():
             z_copy(k).wait_send()
+
+    @pl.when((z > 0) & (z + REACH <= min(NEAR, nz - 1)))
+    def _():
+        relay_copy().wait_send()
+
+    @pl.when(z == 0)
+    def _():
+        for k in list(range(1, min(REACH, nz - 1) + 1)) + far:
+            first_copy(k).wait_send()
 
     for k in range(1, ny):
         y_copy(k, y, (y + k) % ny).wait_send()
@@ -523,6 +596,8 @@
             dma,
             dma((ROW,)),
             dma((ROW,)),
+            pltpu.SemaphoreType.REGULAR((nz,)),
+            dma((nz,)),
             dma((REACH + 1,)),
             dma((REACH + 1,)),
             dma((ROW,)),

time: 33.3 us -> 32 us (0.961)
  Pallas kernels: 31.3 us -> 30 us
    pallas_call x1, Pallas kernels: 31.3 us -> 30 us  [per_device(): pl.pallas_call(functools.partial(main_kernel, nz, ny, tokens, blocks), ou...]
where the time goes in v3:
time: 32 us; the launch traced here: 31.9 us
  Pallas kernels  30 us (94%)
  other arithmetic  1.14 us (4%)
  between operations  0.66 us (2%)
    pallas_call x1, Pallas kernels, per_device(): pl.pallas_call(functools.partial(main_kernel, nz, ny, tokens, blocks), ou...  30 us
    convert_element_type x1, other arithmetic, per_device(): normed = (summed * inv[:, :1] * gain[None, :]).astype(BF16)  1.14 us

profile of v3, /device:TPU:704, one launch (start us, length us, event | category | flops | bytes accessed | tf_op | source)
XLA Modules:
  0.0 31.9 jit_solution(13785545841577870517)
XLA Ops:
  0.6 0.0 copy-start
  0.6 30.0 %scan_conv.1 = (f32[256,1024]{1,0:T(8,128)S(1)}, f32[256,128]{1,0:T(8,128)S(1)}) custom-call(bf16[3,256,1024]{2,1,0:T(8,128)(2,1)} %proj_hbm.1, bf16[256,1024]{1,0:T(8,128)(2,1)} %resid_hbm.1, bf16[3,3,1024]{2,1,0:T(4,128)(2,1)} %weight_hbm.1, f32[16,64]{1,0:T(8,128)} %bitcast.3, f32[16,64]{1,0:T(8,128)} %bitcast.4, f32[1,1024]{1,0:T(1,128)} %bitcast.5), custom_call_target="tpu_custom_call" | custom-call | tf_op jit(solution)/shard_map/scan_conv/pallas_call | solution.py:557
  30.6 0.1 slice_reduce_fusion
  30.7 0.0 copy-done
  30.8 1.1 %multiply_convert_fusion = (bf16[256,1024]{1,0:T(8,128)(2,1)}, bf16[256,1024]{1,0:T(8,128)(2,1)}) fusion(f32[256,1024]{1,0:T(8,128)S(1)} %get-tuple-element.4, f32[1024]{0:T(1024)S(1)} %copy-done, f32[256]{0:T(256)S(1)} %slice_reduce_fusion), kind=kLoop, calls=%fused_computation | loop fusion | flops 1048576 | bytes 2102272 | tf_op jit(solution)/shard_map/convert_element_type | solution.py:626
Async XLA Ops:
  0.6 30.1 %copy-start = (f32[1024]{0:T(1024)S(1)}, f32[1024]{0:T(1024)}, u32[]{:S(2)}) copy-start(f32[1024]{0:T(1024)} %param.13) | copy-start | bytes 12292

commit v4 on v3

--- a/solution.py
+++ b/solution.py
@@ -17,6 +17,8 @@
 BF16 = jnp.bfloat16
 MESH = pl.DeviceIdType.MESH
 REACH = 3
+CHIPS = ROW // 2
+RING = [(step, core) for step in (2, 1, 3) for core in (0, 1)]
 NEAR = 7
 LOCAL_A = 1
 LOCAL_B = 4
@@ -102,7 +104,6 @@
     z_buf,
     x_out,
     x_buf,
-    sq_acc,
     sq_out,
     sq_buf,
     load_sem,
@@ -126,9 +127,20 @@
     z = ctx // ROW
     me = ctx % ROW
     last = nz * ROW - 1
+    partner = me + 1 - 2 * (me % 2)
+    peers = [((me // 2 + step) % CHIPS) * 2 + core for step, core in RING] + [partner]
+    ring = sorted(range(1, ny), key=lambda k: -min(k, ny - k))
+    halves = [pl.ds(h * (width // 2), width // 2) for h in range(2)]
     loads = [
-        pltpu.make_async_copy(proj_hbm.at[c], proj.at[c], load_sem.at[c]) for c in (1, 2, 0)
-    ] + [pltpu.make_async_copy(resid_hbm, resid, load_sem.at[3])]
+        pltpu.make_async_copy(
+            proj_hbm.at[c, :, part], proj.at[c, :, part], load_sem.at[8 + 2 * h + c - 1]
+        )
+        for h, part in enumerate(halves)
+        for c in (1, 2)
+    ] + [
+        pltpu.make_async_copy(proj_hbm.at[0], proj.at[0], load_sem.at[0]),
+        pltpu.make_async_copy(resid_hbm, resid, load_sem.at[3]),
+    ]
     small = [
         pltpu.make_async_copy(src, dst, load_sem.at[4 + k])
         for k, (src, dst) in enumerate(
@@ -140,7 +152,7 @@
             )
         )
     ]
-    for load in small + loads[:2]:
+    for load in small + loads[:4]:
         load.start()
     barrier = pltpu.get_barrier_semaphore()
 
@@ -189,8 +201,6 @@
     lax.fori_loop(0, blocks, fill_states, 0, unroll=True)
     for load in loads[:2]:
         load.wait()
-    for load in loads[2:]:
-        load.start()
 
     def taps_of(c, cols):
         return [weights[tap, c : c + 1, cols] for tap in range(3)]
@@ -208,6 +218,11 @@
         s_buf[block, pl.ds(0, MODES), :] = jnp.sum(total.reshape(GPB, MODES, LANES), axis=0)
         return carry
 
+    lax.fori_loop(0, blocks // 2, states, 0, unroll=True)
+    for load in loads[2:4]:
+        load.wait()
+    for load in loads[4:]:
+        load.start()
     for c in (1, 2):
         tail = proj[c, tokens - 16 :, :].astype(F32)[14:16]
         head = proj[c, :16, :].astype(F32)[:2]
@@ -216,8 +231,8 @@
             mine = slice(block * LANES, (block + 1) * LANES)
             s_buf[block, pl.ds(MODES + 2 * c - 2, 2), :] = tail[:, mine]
             s_buf[block, pl.ds(MODES + 2 * c + 2, 2), :] = head[:, mine]
-    lax.fori_loop(0, blocks, states, 0, unroll=True)
-    loads[2].wait()
+    lax.fori_loop(blocks // 2, blocks, states, 0, unroll=True)
+    loads[4].wait()
     halo_out[0] = proj[0, tokens - 16 :, :].astype(F32)[14:16]
 
     reach = jnp.minimum(nz - 1 - z, REACH)
@@ -256,8 +271,8 @@
         for k in range(ROW):
             edge_copy(k).start()
 
-    for k in range(1, ROW):
-        rs_copy(k, me, (me + k) % ROW).start()
+    for k, peer in enumerate(peers):
+        rs_copy(k, me, peer).start()
     rs_buf[me] = s_buf[me]
 
     def halo_copy():
@@ -293,7 +308,7 @@
     for block in range(blocks):
         p_buf[block, pl.ds(0, 16), :] = product_top[:, block * LANES : (block + 1) * LANES]
 
-    loads[3].wait()
+    loads[5].wait()
     lag_next = (iota((tokens, 1), 0) + 1).astype(F32)
 
     def local(block, carry):
@@ -334,9 +349,8 @@
     rate = by_channel(mode_column(rates_ref, me))
     one_block = jnp.exp(-rate * float(tokens))
     one_row = jnp.exp(-rate * float(tokens * ROW))
-    for k in range(1, ROW):
-        source = (me + ROW - k) % ROW
-        rs_copy(k, source, me).wait_recv()
+    for k, peer in enumerate(peers):
+        rs_copy(k, peer, me).wait_recv()
 
     @pl.when(z == 0)
     def _():
@@ -460,8 +474,8 @@
             device_id_type=MESH,
         )
 
-    for k in range(1, ROW):
-        x_copy(k, me, (me + k) % ROW).start()
+    for k, peer in enumerate(peers):
+        x_copy(k, me, peer).start()
     x_buf[me] = x_out[me]
     lax.fori_loop(LOCAL_B, blocks, local, 0, unroll=True)
     @pl.when(z == 0)
@@ -470,9 +484,6 @@
             pl.semaphore_wait(ready.at[k], 1)
             first_copy(k).start()
 
-    sq_acc[...] = jnp.zeros_like(sq_acc)
-    for k in range(1, ROW):
-        x_copy(k, (me + ROW - k) % ROW, me).wait_recv()
 
     def finish(block, carry):
         cols = pl.ds(pl.multiple_of(block * LANES, LANES), LANES)
@@ -483,13 +494,15 @@
         )
         summed = base_buf[block] + q_buf[block] * carried
         summed_ref[:, cols] = summed
-        sq_acc[...] += summed * summed
-        return carry
-
-    lax.fori_loop(0, blocks, finish, 0, unroll=True)
+        return carry + summed * summed
+
+    squared = finish(me, jnp.zeros((tokens, LANES), F32))
+    for k, peer in reversed(list(enumerate(peers))):
+        x_copy(k, peer, me).wait_recv()
+        squared = finish(peer, squared)
     ones = jnp.ones((8, LANES), BF16)
     contract = (((1,), (1,)), ((), ()))
-    high, low = split(sq_acc[...])
+    high, low = split(squared)
     squares = lax.dot_general(ones, high, contract, preferred_element_type=F32) + lax.dot_general(
         ones, low, contract, preferred_element_type=F32
     )
@@ -505,7 +518,7 @@
             device_id_type=MESH,
         )
 
-    for k in range(1, ny):
+    for k in ring:
         y_copy(k, y, (y + k) % ny).start()
     sq_buf[y] = sq_out[...]
 
@@ -526,9 +539,9 @@
         for k in range(ROW):
             edge_copy(k).wait_send()
 
-    for k in range(1, ROW):
-        rs_copy(k, me, (me + k) % ROW).wait_send()
-        x_copy(k, me, (me + k) % ROW).wait_send()
+    for k, peer in enumerate(peers):
+        rs_copy(k, me, peer).wait_send()
+        x_copy(k, me, peer).wait_send()
     for k in range(1, REACH + 1):
 
         @pl.when((z > 0) & (z + k < nz))
@@ -587,10 +600,9 @@
             pltpu.VMEM((REACH + 1, MODES, LANES), F32),
             pltpu.VMEM((ROW, MODES, LANES), BF16),
             pltpu.VMEM((ROW, MODES, LANES), BF16),
-            pltpu.VMEM((tokens, LANES), F32),
             pltpu.VMEM((1, tokens), F32),
             pltpu.VMEM((ny, 1, tokens), F32),
-            dma((8,)),
+            dma((12,)),
             dma((2,)),
             dma((ROW,)),
             dma,

time: 32 us -> 32.3 us (level)
  no operation moved by 1% of the time
where the time goes in v4:
time: 32.3 us; the launch traced here: 32.1 us
  Pallas kernels  30.2 us (93%)
  other arithmetic  1.14 us (4%)
  between operations  0.66 us (2%)
    pallas_call x1, Pallas kernels, per_device(): pl.pallas_call(functools.partial(main_kernel, nz, ny, tokens, blocks), ou...  30.2 us
    convert_element_type x1, other arithmetic, per_device(): normed = (summed * inv[:, :1] * gain[None, :]).astype(BF16)  1.14 us

profile of v4, /device:TPU:704, one launch (start us, length us, event | category | flops | bytes accessed | tf_op | source)
XLA Modules:
  0.0 32.1 jit_solution(5313518425283296348)
XLA Ops:
  0.6 0.0 copy-start
  0.6 30.2 %scan_conv.1 = (f32[256,1024]{1,0:T(8,128)S(1)}, f32[256,128]{1,0:T(8,128)S(1)}) custom-call(bf16[3,256,1024]{2,1,0:T(8,128)(2,1)} %proj_hbm.1, bf16[256,1024]{1,0:T(8,128)(2,1)} %resid_hbm.1, bf16[3,3,1024]{2,1,0:T(4,128)(2,1)} %weight_hbm.1, f32[16,64]{1,0:T(8,128)} %bitcast.3, f32[16,64]{1,0:T(8,128)} %bitcast.4, f32[1,1024]{1,0:T(1,128)} %bitcast.5), custom_call_target="tpu_custom_call" | custom-call | tf_op jit(solution)/shard_map/scan_conv/pallas_call | solution.py:570
  30.8 0.1 slice_reduce_fusion
  30.9 0.0 copy-done
  30.9 1.1 %multiply_convert_fusion = (bf16[256,1024]{1,0:T(8,128)(2,1)}, bf16[256,1024]{1,0:T(8,128)(2,1)}) fusion(f32[256,1024]{1,0:T(8,128)S(1)} %get-tuple-element.4, f32[1024]{0:T(1024)S(1)} %copy-done, f32[256]{0:T(256)S(1)} %slice_reduce_fusion), kind=kLoop, calls=%fused_computation | loop fusion | flops 1048576 | bytes 2102272 | tf_op jit(solution)/shard_map/convert_element_type | solution.py:638
Async XLA Ops:
  0.6 30.3 %copy-start = (f32[1024]{0:T(1024)S(1)}, f32[1024]{0:T(1024)}, u32[]{:S(2)}) copy-start(f32[1024]{0:T(1024)} %param.13) | copy-start | bytes 12292
